TPU v7x, 32 devices: a whole 2x2x4 slice. The times are simulated.
32 devices in a mesh: row: 8 (over z, y), col: 4 (over x, core).
Axes of the slice: x: 2, y: 2, z: 4, core: 2. Of those that a mesh axis runs over, the one named last changes fastest.
Arguments:
- queries: bfloat16 [1024, 1024], P('row', 'col'), may hold values from -26 to 26
- key_vectors: bfloat16 [1024, 1024], P('row', 'col'), may hold values from -8 to 8
- values: bfloat16 [1024, 1024], P('row', 'col'), may hold values from -6 to 6
- sink_logit: float32 [8], P('col'), may hold values from -1 to 5
- lengths: int32 [8], replicated, may hold values from 1 to 576, as said below
- stream: bfloat16 [1024, 2048], P('row', 'col'), may hold values from -60 to 60
- out_weight: bfloat16 [1024, 2048], P('col', 'row'), may hold values from -0.1875 to 0.1875
- norm_gain: bfloat16 [2048], P('col'), may hold values from 0.25 to 1.75
- shared_gate: bfloat16 [2048, 2816], P('row', 'col'), may hold values from -0.125 to 0.125
- shared_up: bfloat16 [2048, 2816], P('row', 'col'), may hold values from -0.125 to 0.125
- shared_down: bfloat16 [2816, 2048], P('col', 'row'), may hold values from -0.109375 to 0.109375
- shared_switch: bfloat16 [2048], replicated, may hold values from -0.125 to 0.125
- expert_gate: bfloat16 [8, 2048, 1408], P('row', None, 'col'), may hold values from -0.125 to 0.125
- expert_up: bfloat16 [8, 2048, 1408], P('row', None, 'col'), may hold values from -0.125 to 0.125
- expert_down: bfloat16 [8, 1408, 2048], P('row', 'col'), may hold values from -0.15625 to 0.15625
- routes: int32 [1024, 4], P('row'), may hold values from 0 to 7, all different within a row; in each aligned block of 128 rows (0 to 127, 128 to 255, ...) at most 96 rows name the same one
- route_weights: float32 [1024, 4], P('row'), may hold values from 0.05 to 0.6
Outputs:
- attended: bfloat16 [1024, 1024], P('row', 'col')
- layer_out: bfloat16 [1024, 2048], P('row', 'col')
Inputs may be any that keep to these rules, and one draw needn't show every extreme that they name: `routes`: each row names 4 different experts; among the 128 rows of one device (aligned blocks) no expert is named more than 96 times, a bound that some block reaches. The lengths sum to 1024; exactly one prompt has 576 tokens.
All inputs are finite; a program needn't handle non-finite values.
Results may differ from a plain program's by a relative error of at most 0.01.
Values may be sent and summed in bfloat16 or wider, within the bound.
A program may use at most 128 MiB of HBM per device.

v0:
```python
import math
import jax
import jax.numpy as jnp
from jax import lax
from jax.sharding import PartitionSpec as P

HDIM = 128
WINDOW = 4096
norm_eps = 1e-06
masked_score = -1e30


def lower_bounds(lengths, positions):
    doc_ends = jnp.cumsum(lengths)
    starts = doc_ends - lengths
    begun_docs = starts[None, :] <= positions[:, None]
    doc_start = jnp.max(jnp.where(begun_docs, starts[None, :], 0), axis=1)
    return jnp.maximum(doc_start, positions - WINDOW + 1)


def body(
    queries,
    key_vectors,
    values,
    sink_logit,
    lengths,
    stream,
    out_weight,
    norm_gain,
    shared_gate,
    shared_up,
    shared_down,
    shared_switch,
    expert_gate,
    expert_up,
    expert_down,
    routes,
    route_weights,
):
    local_tokens = queries.shape[0]
    feature_width = queries.shape[1]
    head_count = feature_width // HDIM
    my_row = lax.axis_index("row")
    positions = my_row * local_tokens + jnp.arange(local_tokens, dtype=jnp.int32)
    lower_bound = lower_bounds(lengths, positions)
    query_heads = queries.reshape(local_tokens, head_count, HDIM)
    score_scale = 1.0 / math.sqrt(HDIM)
    key_value = jnp.stack([key_vectors, values], 0)
    key_piece = lax.all_gather(key_value, "row", axis=1, tiled=True)
    row_max = jnp.broadcast_to(sink_logit[None, :], (local_tokens, head_count))
    denominator = jnp.ones((local_tokens, head_count), jnp.float32)
    numerator = jnp.zeros((local_tokens, head_count, HDIM), jnp.float32)
    needed = key_piece.shape[1]
    key_heads = key_piece[0].reshape(needed, head_count, HDIM)
    value_heads = key_piece[1].reshape(needed, head_count, HDIM)
    scores = (
        jnp.einsum("qhd,khd->qhk", query_heads, key_heads, preferred_element_type=jnp.float32)
        * score_scale
    )
    key_places = jnp.arange(needed, dtype=jnp.int32)
    visible = (
        (key_places[None, :] >= lower_bound[:, None]) & (key_places[None, :] <= positions[:, None])
    )[:, None, :]
    masked = jnp.where(visible, scores, masked_score)
    new_max = jnp.maximum(row_max, jnp.max(masked, axis=2))
    weight = jnp.where(visible, jnp.exp(masked - new_max[:, :, None]), 0.0)
    rescale = jnp.exp(row_max - new_max)
    denominator = denominator * rescale + jnp.sum(weight, axis=2)
    numerator = numerator * rescale[:, :, None] + jnp.einsum(
        "qhk,khd->qhd", weight.astype(jnp.bfloat16), value_heads, preferred_element_type=jnp.float32
    )
    final_max, denominator, numerator = (new_max, denominator, numerator)
    attended = (
        (numerator / denominator[:, :, None])
        .reshape(local_tokens, feature_width)
        .astype(jnp.bfloat16)
    )
    head_terms = jnp.dot(
        attended,
        lax.all_gather(out_weight, "row", axis=1, tiled=True),
        preferred_element_type=jnp.float32,
    )
    mixed_heads = lax.psum_scatter(
        head_terms.astype(jnp.bfloat16), "col", scatter_dimension=1, tiled=True
    ).astype(jnp.float32)
    hidden = (stream.astype(jnp.float32) + mixed_heads).astype(jnp.bfloat16)
    widened = hidden.astype(jnp.float32)
    full_width = lax.axis_size("col") * hidden.shape[1]
    squares = lax.psum(jnp.sum(widened * widened, axis=1), "col")
    row_scale = lax.rsqrt(squares / full_width + norm_eps)
    normed_part = (widened * row_scale[:, None] * norm_gain.astype(jnp.float32)).astype(
        jnp.bfloat16
    )
    normed = lax.all_gather(normed_part, "col", axis=1, tiled=True)
    gate_part = jnp.dot(
        normed,
        lax.all_gather(shared_gate, "row", axis=0, tiled=True),
        preferred_element_type=jnp.float32,
    )
    up_part = jnp.dot(
        normed,
        lax.all_gather(shared_up, "row", axis=0, tiled=True),
        preferred_element_type=jnp.float32,
    )
    shared_act = (jax.nn.silu(gate_part) * up_part).astype(jnp.bfloat16)
    shared_part = jnp.dot(
        shared_act,
        lax.all_gather(shared_down, "row", axis=1, tiled=True),
        preferred_element_type=jnp.float32,
    )
    switch = jax.nn.sigmoid(jnp.dot(normed, shared_switch, preferred_element_type=jnp.float32))
    row_count = lax.axis_size("row")
    fanout = routes.shape[1]
    model_width = normed.shape[1]
    capacity = max(2, min(local_tokens, 3 * local_tokens * fanout // (2 * row_count)))
    flat_routes = routes.reshape(-1)
    onehot = (flat_routes[:, None] == jnp.arange(row_count, dtype=jnp.int32)[None, :]).astype(
        jnp.int32
    )
    before = jnp.cumsum(onehot, axis=0) - onehot
    slot_index = jnp.sum(before * onehot, axis=1)
    target = flat_routes * capacity + slot_index
    owner_row = jnp.arange(local_tokens * fanout, dtype=jnp.int32) // fanout
    source = jnp.full((row_count * capacity,), local_tokens, jnp.int32).at[target].set(owner_row)
    padded = jnp.concatenate([normed, jnp.zeros((1, model_width), jnp.bfloat16)], 0)
    outgoing = padded[source].reshape(row_count, capacity, model_width)
    received = lax.all_to_all(outgoing, "row", split_axis=0, concat_axis=0, tiled=True)
    senders, slot_count, received_width = received.shape
    dispatched = received.reshape(senders * slot_count, received_width)
    gate_out = jnp.dot(dispatched, expert_gate[0], preferred_element_type=jnp.float32)
    up_out = jnp.dot(dispatched, expert_up[0], preferred_element_type=jnp.float32)
    activation = (jax.nn.silu(gate_out) * up_out).astype(jnp.bfloat16)
    partial_out = jnp.dot(activation, expert_down[0], preferred_element_type=jnp.float32).astype(
        jnp.bfloat16
    )
    returned = lax.all_to_all(
        partial_out.reshape(senders, slot_count, received_width),
        "row",
        split_axis=0,
        concat_axis=0,
        tiled=True,
    )
    route_rows = returned.reshape(row_count * capacity, model_width)[target].reshape(
        local_tokens, fanout, model_width
    )
    routed = jnp.zeros((local_tokens, model_width), jnp.float32)
    for route_slot in range(fanout):
        routed = routed + route_weights[:, route_slot][:, None] * route_rows[
            :, route_slot, :
        ].astype(jnp.float32)
    layer_terms = switch[:, None] * shared_part + routed
    summed = lax.psum_scatter(
        layer_terms.astype(jnp.bfloat16), "col", scatter_dimension=1, tiled=True
    ).astype(jnp.float32)
    layer_out = (hidden.astype(jnp.float32) + summed).astype(jnp.bfloat16)
    return (attended, layer_out)


def solution(mesh):
    return jax.shard_map(
        body,
        mesh=mesh,
        in_specs=(
            P("row", "col"),
            P("row", "col"),
            P("row", "col"),
            P("col"),
            P(),
            P("row", "col"),
            P("col", "row"),
            P("col"),
            P("row", "col"),
            P("row", "col"),
            P("col", "row"),
            P(),
            P("row", None, "col"),
            P("row", None, "col"),
            P("row", "col", None),
            P("row", None),
            P("row", None),
        ),
        out_specs=(P("row", "col"), P("row", "col")),
        check_vma=False,
    )
```

profile of v0, /device:TPU:0, one launch (start us, length us, event | category | flops | bytes accessed | tf_op | source)
XLA Modules:
  0.0 430.8 jit_solution(6506192966484894538)
XLA Ops:
  7.2 0.0 copy-start
  7.2 0.0 all-gather.6.cloned.1.call-start
  7.2 1.1 copy.36
  8.3 1.0 copy.37
  9.3 0.7 pad_maximum_fusion
  9.9 0.0 all-gather.6.cloned.1.call-update
  10.0 0.0 all-gather.8.cloned.1.call-start
  10.0 0.7 all-gather.8.cloned.1.call-update
  10.7 0.0 reduce-scatter.3.cloned.1.call-start
  10.8 0.8 reduce-window.19
  11.6 0.7 bitcast_subtract_fusion.1
  12.3 0.1 select_reduce_fusion
  12.4 0.1 fusion.34
  12.5 40.4 %all-gather.6.cloned.1.call-done = bf16[2,1024,256]{1,2,0:T(8,128)(2,1)} async-done(((bf16[2,128,256]{1,2,0:T(8,128)(2,1)}), bf16[2,1024,256]{1,2,0:T(8,128)(2,1)}) %all-gather.6.cloned.1.call-update) | async-done | bytes 1048592 | tf_op jit(solution)/shard_map/all_gather | solution.py:49
  52.9 1.3 fusion.62
  54.2 0.4 fusion.63
  54.6 0.1 broadcast_maximum_fusion
  54.6 0.2 fusion.28
  54.9 0.1 fusion.57
  55.0 0.4 fusion.18
  55.4 0.0 copy-start.2
  55.4 38.0 %all-gather.8.cloned.1.call-done = bf16[256,2048]{1,0:T(8,128)(2,1)} async-done(((bf16[256,256]{1,0:T(8,128)(2,1)}), bf16[256,2048]{1,0:T(8,128)(2,1)}) %all-gather.8.cloned.1.call-update) | async-done | bytes 1048592 | tf_op jit(solution)/shard_map/all_gather | solution.py:80
  93.4 2.4 convolution_convert_fusion.1
  95.8 0.0 reduce-scatter.3.cloned.1.call-update
  95.8 0.0 all-gather.10.cloned.1.call-start
  95.9 0.5 all-gather.10.cloned.1.call-update
  96.4 0.1 copy.42
  96.5 0.1 eq.29
  96.6 0.1 eq.25
  96.8 1.1 reduce-window.20
  97.9 0.2 slice_reduce_fusion
  98.2 0.1 copy.41
  98.3 0.1 mul.135
  98.4 0.1 fusion.49
  98.5 2.4 scatter_custom_fusion
  101.0 15.5 %reduce-scatter.3.cloned.1.call-done = bf16[128,512]{1,0:T(8,128)(2,1)} async-done(((bf16[128,2048]{1,0:T(8,128)(2,1)}), bf16[128,512]{1,0:T(8,128)(2,1)}) %reduce-scatter.3.cloned.1.call-update) | async-done | bytes 131088 | tf_op jit(solution)/shard_map/reduce_scatter | solution.py:83
  116.5 1.0 fusion.41
  117.5 5.8 %psum.7 = f32[128]{0:T(128)S(1)} all-reduce(f32[128]{0:T(128)S(1)} %fusion.41), channel_id=1, replica_groups=mesh['row'=8,'col'=4] {'col'}, use_global_device_ids=true, to_apply=%region_6.7 | all-reduce | flops 128 | bytes 1024 | tf_op jit(solution)/shard_map/psum | solution.py:89
  123.3 1.0 fusion.43
  124.3 7.3 %all_gather.20 = bf16[128,2048]{1,0:T(8,128)(2,1)S(1)} all-gather(bf16[128,512]{1,0:T(8,128)(2,1)S(1)} %fusion.43), channel_id=1, replica_groups=mesh['row'=8,'col'=4] {'col'}, dimensions={1}, use_global_device_ids=true | all-gather | bytes 655360 | tf_op jit(solution)/shard_map/all_gather | solution.py:94
  131.7 4.3 gather_fusion
  135.9 5.5 %all-to-all-start = ((bf16[8,96,2048]{2,1,0:T(8,128)(2,1)}), bf16[8,96,2048]{2,1,0:T(8,128)(2,1)}, u32[]{:S(2)}, u32[]{:S(2)}) async-start(bf16[8,96,2048]{2,1,0:T(8,128)(2,1)} %bitcast.109), calls=%async_computation.1 | async-start | bytes 6291456 | tf_op jit(solution)/shard_map/all_to_all | solution.py:127
  141.5 0.0 all-gather.12.cloned.1.call-start
  141.5 0.5 all-gather.12.cloned.1.call-update
  142.1 94.2 %all-to-all-done = bf16[8,96,2048]{2,1,0:T(8,128)(2,1)} async-done(((bf16[8,96,2048]{2,1,0:T(8,128)(2,1)}), bf16[8,96,2048]{2,1,0:T(8,128)(2,1)}, u32[]{:S(2)}, u32[]{:S(2)}) %all-to-all-start) | async-done | bytes 3145760 | tf_op jit(solution)/shard_map/all_to_all | solution.py:127
  236.2 4.7 %fusion.5 = f32[768,352]{0,1:T(8,128)} fusion(bf16[768,2048]{1,0:T(8,128)(2,1)} %bitcast.16, bf16[1,2048,352]{1,2,0:T(8,128)(2,1)} %param.29), kind=kOutput, calls=%fused_computation.11 | convolution fusion | flops 1107296256 | bytes 5668864 | tf_op jit(solution)/shard_map/dot_general | solution.py:130
  240.9 8.0 %convolution_convert_fusion = bf16[768,2048]{1,0:T(8,128)(2,1)} fusion(bf16[1,352,2048]{2,1,0:T(8,128)(2,1)S(1)} %copy-done, bf16[768,2048]{1,0:T(8,128)(2,1)} %bitcast.16, bf16[1,2048,352]{1,2,0:T(8,128)(2,1)} %param.30, f32[768,352]{0,1:T(8,128)} %fusion.5), kind=kOutput, calls=%fused_computation.3 | convolution fusion | flops 2217787392 | bytes 10256384 | tf_op jit(solution)/shard_map/dot_general | solution.py:133
  248.9 4.6 %all-to-all-start.1 = ((bf16[8,96,2048]{2,1,0:T(8,128)(2,1)}), bf16[8,96,2048]{2,1,0:T(8,128)(2,1)}, u32[]{:S(2)}, u32[]{:S(2)}) async-start(bf16[8,96,2048]{2,1,0:T(8,128)(2,1)} %bitcast.110), calls=%async_computation.2 | async-start | bytes 6291456 | tf_op jit(solution)/shard_map/all_to_all | solution.py:136
  253.5 0.0 all-gather.14.cloned.1.call-start
  253.6 0.5 all-gather.14.cloned.1.call-update
  254.1 0.2 reduce-scatter.5.cloned.1.call-start
  254.4 0.5 slice_bitcast_fusion.3
  254.9 0.3 fusion.22
  255.1 3.5 fusion.64
  258.6 92.9 %all-to-all-done.1 = bf16[8,96,2048]{2,1,0:T(8,128)(2,1)} async-done(((bf16[8,96,2048]{2,1,0:T(8,128)(2,1)}), bf16[8,96,2048]{2,1,0:T(8,128)(2,1)}, u32[]{:S(2)}, u32[]{:S(2)}) %all-to-all-start.1) | async-done | bytes 3145760 | tf_op jit(solution)/shard_map/all_to_all | solution.py:136
  351.5 7.5 %gather_fusion.1 = bf16[512,2048]{1,0:T(8,128)(2,1)} fusion(bf16[768,2048]{1,0:T(8,128)(2,1)} %bitcast.21, s32[1024]{0:T(1024)S(1)} %pad_clamp_fusion), kind=kCustom, calls=%fused_computation.1 | custom fusion | bytes 4196352 | tf_op jit(solution)/shard_map/gather | solution.py:143
  359.0 2.7 reshape.220
  361.8 4.5 %fusion.61 = (bf16[128,1,2048]{2,1,0:T(2,128)(2,1)}, bf16[128,1,2048]{2,1,0:T(2,128)(2,1)}, bf16[128,1,2048]{2,1,0:T(2,128)(2,1)}, bf16[128,1,2048]{2,1,0:T(2,128)(2,1)}) fusion(bf16[128,4,2048]{2,1,0:T(4,128)(2,1)S(1)} %reshape.220), kind=kLoop, calls=%fused_computation.104 | loop fusion | bytes 4194304 | tf_op jit(solution)/shard_map/slice | solution.py:148
  366.3 27.9 %all-gather.14.cloned.1.call-done = bf16[704,2048]{1,0:T(8,128)(2,1)} async-done(((bf16[704,256]{1,0:T(8,128)(2,1)}), bf16[704,2048]{1,0:T(8,128)(2,1)}) %all-gather.14.cloned.1.call-update) | async-done | bytes 2883600 | tf_op jit(solution)/shard_map/all_gather | solution.py:108
  394.2 8.1 %fusion.1 = bf16[128,2048]{1,0:T(8,128)(2,1)} fusion(bf16[704,2048]{1,0:T(8,128)(2,1)} %all-gather.14.cloned.1.call-done, bf16[128,2048]{1,0:T(8,128)(2,1)} %copy-done.1, bf16[2048,704]{0,1:T(8,128)(2,1)} %all-gather.12.cloned.1.call-done, bf16[128,1,2048]{2,1,0:T(2,128)(2,1)} %get-tuple-element.11, bf16[128,1,2048]{2,1,0:T(2,128)(2,1)} %get-tuple-element.9, ...), kind=kOutput, calls=%fused_computation.6 | convolution fusion | flops 742408192 | bytes 9275904 | tf_op jit(solution)/shard_map/dot_general | solution.py:106
  402.3 0.0 reduce-scatter.5.cloned.1.call-update
  402.3 0.7 copy.48
  403.1 19.3 %reduce-scatter.5.cloned.1.call-done = bf16[128,512]{1,0:T(8,128)(2,1)} async-done(((bf16[128,2048]{1,0:T(8,128)(2,1)}), bf16[128,512]{1,0:T(8,128)(2,1)}) %reduce-scatter.5.cloned.1.call-update) | async-done | bytes 131088 | tf_op jit(solution)/shard_map/reduce_scatter | solution.py:152
  422.3 1.6 fusion.44
  (41 shorter events, 0.2 us)
Async XLA Ops:
  7.2 233.7 %copy-start = (bf16[1,352,2048]{2,1,0:T(8,128)(2,1)S(1)}, bf16[1,352,2048]{2,1,0:T(8,128)(2,1)}, u32[]{:S(2)}) copy-start(bf16[1,352,2048]{2,1,0:T(8,128)(2,1)} %param.31) | copy-start | bytes 4325380
  7.2 47.0 %copy-start.7 = (bf16[128,256]{1,0:T(8,128)(2,1)S(1)}, bf16[128,256]{1,0:T(8,128)(2,1)}, u32[]{:S(2)}) copy-start(bf16[128,256]{1,0:T(8,128)(2,1)} %param.17) | copy-start | bytes 196612
  7.2 45.7 %all-gather.6.cloned.1.call-start = ((), (), s32[]{:S(2)}) async-start(), calls=%async_computation.4 | async-start | bytes 1179648 | tf_op jit(solution)/shard_map/all_gather | solution.py:49
  10.0 44.6 %copy-start.10 = (f32[2]{0:T(128)S(1)}, f32[2]{0:T(128)}, u32[]{:S(2)}) copy-start(f32[2]{0:T(128)} %param.20) | copy-start | bytes 28
  10.0 83.4 %all-gather.8.cloned.1.call-start = ((), (), s32[]{:S(2)}) async-start(), calls=%async_computation.5 | async-start | bytes 1179648 | tf_op jit(solution)/shard_map/all_gather | solution.py:80
  10.7 105.8 %reduce-scatter.3.cloned.1.call-start = ((), (), s32[]{:S(2)}) async-start(), calls=%async_computation.6 | async-start | bytes 655360 | tf_op jit(solution)/shard_map/reduce_scatter | solution.py:83
  54.9 41.4 %copy-start.8 = (s32[128,4]{0,1:T(4,128)S(1)}, s32[128,4]{0,1:T(4,128)}, u32[]{:S(2)}) copy-start(s32[128,4]{0,1:T(4,128)} %param.32) | copy-start | bytes 6148
  54.9 41.8 %copy-start.12 = (bf16[512]{0:T(512)(128)(2,1)S(1)}, bf16[512]{0:T(512)(128)(2,1)}, u32[]{:S(2)}) copy-start(bf16[512]{0:T(512)(128)(2,1)} %param.24) | copy-start | bytes 3076
  55.3 40.5 %copy-start.5 = (bf16[128,2,128]{0,2,1:T(8,128)(2,1)}, bf16[128,2,128]{0,2,1:T(8,128)(2,1)S(1)}, u32[]{:S(2)}) copy-start(bf16[128,2,128]{0,2,1:T(8,128)(2,1)S(1)} %fusion.18) | copy-start | bytes 196612
  55.4 61.1 %copy-start.2 = (bf16[128,512]{1,0:T(8,128)(2,1)S(1)}, bf16[128,512]{1,0:T(8,128)(2,1)}, u32[]{:S(2)}) copy-start(bf16[128,512]{1,0:T(8,128)(2,1)} %param.22) | copy-start | bytes 393220
  95.8 159.3 %all-gather.10.cloned.1.call-start = ((), (), s32[]{:S(2)}) async-start(), calls=%async_computation.7 | async-start | bytes 3244032 | tf_op jit(solution)/shard_map/all_gather | solution.py:97
  131.6 123.5 %copy-start.1 = (bf16[128,2048]{1,0:T(8,128)(2,1)}, bf16[128,2048]{1,0:T(8,128)(2,1)S(1)}, u32[]{:S(2)}) copy-start(bf16[128,2048]{1,0:T(8,128)(2,1)S(1)} %all_gather.20) | copy-start | bytes 1572868
  135.9 100.3 %all-to-all-start = ((bf16[8,96,2048]{2,1,0:T(8,128)(2,1)}), bf16[8,96,2048]{2,1,0:T(8,128)(2,1)}, u32[]{:S(2)}, u32[]{:S(2)}) async-start(bf16[8,96,2048]{2,1,0:T(8,128)(2,1)} %bitcast.109), calls=%async_computation.1 | async-start | bytes 6291456 | tf_op jit(solution)/shard_map/all_to_all | solution.py:127
  141.5 224.8 %all-gather.12.cloned.1.call-start = ((), (), s32[]{:S(2)}) async-start(), calls=%async_computation.8 | async-start | bytes 3244032 | tf_op jit(solution)/shard_map/all_gather | solution.py:102
  248.9 5.4 %copy-start.9 = (bf16[2048]{0:T(1024)(128)(2,1)S(1)}, bf16[2048]{0:T(1024)(128)(2,1)}, u32[]{:S(2)}) copy-start(bf16[2048]{0:T(1024)(128)(2,1)} %param.28) | copy-start | bytes 12292
  248.9 5.4 %copy-start.11 = (f32[128,4]{0,1:T(4,128)S(1)}, f32[128,4]{0,1:T(4,128)}, u32[]{:S(2)}) copy-start(f32[128,4]{0,1:T(4,128)} %param.33) | copy-start | bytes 6148
  248.9 102.6 %all-to-all-start.1 = ((bf16[8,96,2048]{2,1,0:T(8,128)(2,1)}), bf16[8,96,2048]{2,1,0:T(8,128)(2,1)}, u32[]{:S(2)}, u32[]{:S(2)}) async-start(bf16[8,96,2048]{2,1,0:T(8,128)(2,1)} %bitcast.110), calls=%async_computation.2 | async-start | bytes 6291456 | tf_op jit(solution)/shard_map/all_to_all | solution.py:136
  253.5 140.7 %all-gather.14.cloned.1.call-start = ((), (), s32[]{:S(2)}) async-start(), calls=%async_computation.9 | async-start | bytes 3244032 | tf_op jit(solution)/shard_map/all_gather | solution.py:108
  254.1 168.3 %reduce-scatter.5.cloned.1.call-start = ((), (), s32[]{:S(2)}) async-start(), calls=%async_computation.10 | async-start | bytes 655360 | tf_op jit(solution)/shard_map/reduce_scatter | solution.py:152
  394.2 8.1 %copy-start.6 = (bf16[128,2,128]{0,2,1:T(8,128)(2,1)S(1)}, bf16[128,2,128]{0,2,1:T(8,128)(2,1)}, u32[]{:S(2)}) copy-start(bf16[128,2,128]{0,2,1:T(8,128)(2,1)} %copy-done.5) | copy-start | bytes 196612
  394.2 28.1 %copy-start.3 = (bf16[128,512]{1,0:T(8,128)(2,1)S(1)}, bf16[128,512]{1,0:T(8,128)(2,1)}, u32[]{:S(2)}) copy-start(bf16[128,512]{1,0:T(8,128)(2,1)} %param.22) | copy-start | bytes 393220
  394.2 28.1 %copy-start.4 = (bf16[128,512]{1,0:T(8,128)(2,1)S(1)}, bf16[128,512]{1,0:T(8,128)(2,1)}, u32[]{:S(2)}) copy-start(bf16[128,512]{1,0:T(8,128)(2,1)} %reduce-scatter.3.cloned.1.call-done) | copy-start | bytes 393220
Sparse Core Ops, SparseCore 0:
  10.6 42.2 all-gather.5
  55.0 38.4 all-gather.7
  95.9 20.5 reduce-scatter.2
  118.6 109.6 all-gather.9
  230.3 102.7 all-gather.11
  335.3 58.9 all-gather.13
  402.4 19.8 reduce-scatter.4
where the time goes:
time: 431 us
  waiting for transfers between devices  330 us (77%)
  matrix products  27.7 us (6%)
  local copies, waits for them, and re-layouts  26.9 us (6%)
  between operations  14.4 us (3%)
  blocking collectives  13.1 us (3%)
  starting transfers between devices  10.6 us (2%)
  other arithmetic  7.72 us (2%)
    all_to_all x1, waiting for transfers between devices, body(): lax.all_to_all(outgoing, 'row', split_axis=0, concat_axis=0, tiled=True)  94.2 us
    all_to_all x1, waiting for transfers between devices, body(): lax.all_to_all(partial_out.reshape(senders, slot_count, received_width),...  92.9 us
    all_gather x1, waiting for transfers between devices, body(): key_piece = lax.all_gather(key_value, 'row', axis=1, tiled=True)  40.4 us
    all_gather x1, waiting for transfers between devices, body(): lax.all_gather(out_weight, 'row', axis=1, tiled=True)  38 us
    all_gather x1, waiting for transfers between devices, body(): lax.all_gather(shared_down, 'row', axis=1, tiled=True)  27.9 us
    reduce_scatter x1, waiting for transfers between devices, body(): lax.psum_scatter(layer_terms.astype(jnp.bfloat16), 'col', scatter_dimensi...  19.3 us
    reduce_scatter x1, waiting for transfers between devices, body(): lax.psum_scatter(head_terms.astype(jnp.bfloat16), 'col', scatter_dimensio...  15.5 us
  transfers between devices with their start and end apart: 9, of which 7 were waited for; matrix products, arithmetic and copies ran while one was open for 11% of the time, Pallas kernels for 0%

commit v1 on v0

--- a/solution.py
+++ b/solution.py
@@ -46,7 +46,16 @@
     query_heads = queries.reshape(local_tokens, head_count, HDIM)
     score_scale = 1.0 / math.sqrt(HDIM)
     key_value = jnp.stack([key_vectors, values], 0)
-    key_piece = lax.all_gather(key_value, "row", axis=1, tiled=True)
+    response = lax.axis_size("row")
+    inter = lax.axis_index("row")
+    e_next, work_now, extra = (response, inter, key_value.shape[1])
+    parts_out, r2 = (key_value, 1)
+    while r2 < e_next:
+        n_now = tuple(((w, (w - r2) % e_next) for w in range(e_next)))
+        carry_out = lax.ppermute(parts_out, "row", n_now)
+        parts_out = jnp.concatenate([parts_out, carry_out], 1)
+        r2 = 2 * r2
+    key_piece = jnp.roll(parts_out, work_now * extra, 1)
     row_max = jnp.broadcast_to(sink_logit[None, :], (local_tokens, head_count))
     denominator = jnp.ones((local_tokens, head_count), jnp.float32)
     numerator = jnp.zeros((local_tokens, head_count, HDIM), jnp.float32)

time: 431 us -> 407 us (0.944)
  waiting for transfers between devices: 330 us -> 293 us
  starting transfers between devices: 10.6 us -> 18.1 us
  local copies, waits for them, and re-layouts: 26.9 us -> 31.6 us
    all_gather x1 -> x0, waiting for transfers between devices: 40.4 us -> none  [body(): key_piece = lax.all_gather(key_value, 'row', axis=1, tiled=True)]
    ppermute x0 -> x3, waiting for transfers between devices: none -> 32.1 us  [body(): carry_out = lax.ppermute(parts_out, 'row', n_now)]
    all_gather x1, waiting for transfers between devices: 38 us -> 6.65 us  [body(): lax.all_gather(out_weight, 'row', axis=1, tiled=True)]
    all_gather x1, waiting for transfers between devices: 27.9 us -> 0.01 us  [body(): lax.all_gather(shared_down, 'row', axis=1, tiled=True)]
    all_gather x1, waiting for transfers between devices: 0.01 us -> 27.7 us  [body(): lax.all_gather(shared_up, 'row', axis=0, tiled=True)]
    ppermute x0 -> x3, starting transfers between devices: none -> 7.65 us  [body(): carry_out = lax.ppermute(parts_out, 'row', n_now)]
  transfers between devices with their start and end apart: 9 -> 11, of which waited for: 7 -> 9; matrix products, arithmetic and copies ran while one was open for 11% -> 13% of each run, Pallas kernels for 0% -> 0%
where the time goes in v1:
time: 407 us
  waiting for transfers between devices  293 us (72%)
  local copies, waits for them, and re-layouts  31.6 us (8%)
  matrix products  27.7 us (7%)
  starting transfers between devices  18.1 us (4%)
  between operations  14.4 us (4%)
  blocking collectives  13.1 us (3%)
  other arithmetic  8.49 us (2%)
    all_to_all x1, waiting for transfers between devices, body(): lax.all_to_all(outgoing, 'row', split_axis=0, concat_axis=0, tiled=True)  94.3 us
    all_to_all x1, waiting for transfers between devices, body(): lax.all_to_all(partial_out.reshape(senders, slot_count, received_width),...  93.1 us
    ppermute x3, waiting for transfers between devices, body(): carry_out = lax.ppermute(parts_out, 'row', n_now)  32.1 us
    all_gather x1, waiting for transfers between devices, body(): lax.all_gather(shared_up, 'row', axis=0, tiled=True)  27.7 us
    reduce_scatter x1, waiting for transfers between devices, body(): lax.psum_scatter(layer_terms.astype(jnp.bfloat16), 'col', scatter_dimensi...  19.2 us
    reduce_scatter x1, waiting for transfers between devices, body(): lax.psum_scatter(head_terms.astype(jnp.bfloat16), 'col', scatter_dimensio...  18.6 us
  transfers between devices with their start and end apart: 11, of which 9 were waited for; matrix products, arithmetic and copies ran while one was open for 13% of the time, Pallas kernels for 0%

profile of v1, /device:TPU:0, one launch (start us, length us, event | category | flops | bytes accessed | tf_op | source)
XLA Modules:
  0.0 406.8 jit_solution(2784416721896887481)
XLA Ops:
  7.2 1.1 copy.36
  8.3 1.0 copy.37
  9.2 0.7 pad_maximum_fusion.2
  9.9 6.0 %collective-permute-start = (bf16[2,128,256]{1,2,0:T(8,128)(2,1)S(1)}, bf16[2,128,256]{1,2,0:T(8,128)(2,1)S(1)}, u32[]{:S(2)}, u32[]{:S(2)}) collective-permute-start(bf16[2,128,256]{1,2,0:T(8,128)(2,1)S(1)} %get-tuple-element.14), channel_id=1, source_target_pairs={{0,28},{4,0},{8,4},{12,8},{16,12},{20,16},{24,20},{28,24},{1,29},{... | collective-permute-start | bytes 393224 | tf_op jit(solution)/shard_map/ppermute | solution.py:55
  16.0 0.8 reduce-window.19
  16.8 1.8 collective-permute-done
  18.7 1.6 collective-permute-start.1
  20.3 0.7 bitcast_subtract_fusion.1
  21.0 0.1 select_reduce_fusion
  21.1 8.1 %collective-permute-done.1 = bf16[2,256,256]{1,2,0:T(8,128)(2,1)S(1)} collective-permute-done((bf16[2,256,256]{1,2,0:T(8,128)(2,1)S(1)}, bf16[2,256,256]{1,2,0:T(8,128)(2,1)S(1)}, u32[]{:S(2)}, u32[]{:S(2)}) %collective-permute-start.1) | collective-permute-done | bytes 262176 | tf_op jit(solution)/shard_map/ppermute | solution.py:55
  29.2 0.1 collective-permute-start.2
  29.3 0.1 fusion.34
  29.4 0.7 constant_dynamic-update-slice_fusion.6
  30.1 0.7 constant_dynamic-update-slice_fusion.5
  30.9 22.1 %collective-permute-done.2 = bf16[2,512,256]{1,2,0:T(8,128)(2,1)S(1)} collective-permute-done((bf16[2,512,256]{1,2,0:T(8,128)(2,1)S(1)}, bf16[2,512,256]{1,2,0:T(8,128)(2,1)S(1)}, u32[]{:S(2)}, u32[]{:S(2)}) %collective-permute-start.2) | collective-permute-done | bytes 524320 | tf_op jit(solution)/shard_map/ppermute | solution.py:55
  53.0 0.9 constant_dynamic-update-slice_fusion.4
  53.9 0.7 constant_dynamic-update-slice_fusion.3
  54.6 0.7 constant_dynamic-update-slice_fusion.2
  55.3 0.7 constant_dynamic-update-slice_fusion.1
  56.0 0.9 constant_dynamic-update-slice_fusion
  56.9 1.3 constant_dynamic-slice_fusion
  58.2 0.4 fusion.62
  58.6 0.1 broadcast_maximum_fusion
  58.7 0.2 fusion.28
  58.9 0.1 fusion.57
  59.0 0.4 fusion.18
  59.4 6.7 %all-gather.5.cloned.1.call-done = bf16[256,2048]{1,0:T(8,128)(2,1)} async-done(((bf16[256,256]{1,0:T(8,128)(2,1)}), bf16[256,2048]{1,0:T(8,128)(2,1)}) %all-gather.5.cloned.1.call-update) | async-done | bytes 1048592 | tf_op jit(solution)/shard_map/all_gather | solution.py:89
  66.0 2.4 convolution_convert_fusion.1
  68.5 0.7 all-gather.7.cloned.1.call-update
  69.2 0.1 copy.42
  69.3 0.1 eq.32
  69.4 0.1 eq.28
  69.5 1.1 reduce-window.20
  70.7 0.2 slice_reduce_fusion
  70.9 0.1 copy.41
  71.1 0.1 mul.136
  71.2 0.1 fusion.49
  71.3 2.4 scatter_custom_fusion
  73.8 18.6 %reduce-scatter.3.cloned.1.call-done = bf16[128,512]{1,0:T(8,128)(2,1)} async-done(((bf16[128,2048]{1,0:T(8,128)(2,1)}), bf16[128,512]{1,0:T(8,128)(2,1)}) %reduce-scatter.3.cloned.1.call-update) | async-done | bytes 131088 | tf_op jit(solution)/shard_map/reduce_scatter | solution.py:92
  92.4 1.0 fusion.41
  93.4 5.8 %psum.7 = f32[128]{0:T(128)S(1)} all-reduce(f32[128]{0:T(128)S(1)} %fusion.41), channel_id=1, replica_groups=mesh['row'=8,'col'=4] {'col'}, use_global_device_ids=true, to_apply=%region_6.7 | all-reduce | flops 128 | bytes 1024 | tf_op jit(solution)/shard_map/psum | solution.py:98
  99.2 1.0 fusion.43
  100.2 7.3 %all_gather.16 = bf16[128,2048]{1,0:T(8,128)(2,1)S(1)} all-gather(bf16[128,512]{1,0:T(8,128)(2,1)S(1)} %fusion.43), channel_id=1, replica_groups=mesh['row'=8,'col'=4] {'col'}, dimensions={1}, use_global_device_ids=true | all-gather | bytes 655360 | tf_op jit(solution)/shard_map/all_gather | solution.py:103
  107.6 4.3 %gather_fusion = bf16[768,2048]{1,0:T(8,128)(2,1)} fusion(bf16[129,2048]{1,0:T(8,128)(2,1)S(1)} %concatenate.20, s32[1024]{0:T(1024)S(1)} %pad_clamp_fusion.1), kind=kCustom, calls=%fused_computation | custom fusion | bytes 6294528 | tf_op jit(solution)/shard_map/gather | solution.py:135
  111.8 5.5 %all-to-all-start = ((bf16[8,96,2048]{2,1,0:T(8,128)(2,1)}), bf16[8,96,2048]{2,1,0:T(8,128)(2,1)}, u32[]{:S(2)}, u32[]{:S(2)}) async-start(bf16[8,96,2048]{2,1,0:T(8,128)(2,1)} %bitcast.109), calls=%async_computation.1 | async-start | bytes 6291456 | tf_op jit(solution)/shard_map/all_to_all | solution.py:136
  117.4 0.5 all-gather.11.cloned.1.call-update
  117.9 94.3 %all-to-all-done = bf16[8,96,2048]{2,1,0:T(8,128)(2,1)} async-done(((bf16[8,96,2048]{2,1,0:T(8,128)(2,1)}), bf16[8,96,2048]{2,1,0:T(8,128)(2,1)}, u32[]{:S(2)}, u32[]{:S(2)}) %all-to-all-start) | async-done | bytes 3145760 | tf_op jit(solution)/shard_map/all_to_all | solution.py:136
  212.2 4.7 %fusion.5 = f32[768,352]{0,1:T(8,128)} fusion(bf16[768,2048]{1,0:T(8,128)(2,1)} %bitcast.16, bf16[1,2048,352]{1,2,0:T(8,128)(2,1)} %param.29), kind=kOutput, calls=%fused_computation.11 | convolution fusion | flops 1107296256 | bytes 5668864 | tf_op jit(solution)/shard_map/dot_general | solution.py:139
  216.9 8.0 %convolution_convert_fusion = bf16[768,2048]{1,0:T(8,128)(2,1)} fusion(bf16[1,352,2048]{2,1,0:T(8,128)(2,1)S(1)} %copy-done, bf16[768,2048]{1,0:T(8,128)(2,1)} %bitcast.16, bf16[1,2048,352]{1,2,0:T(8,128)(2,1)} %param.30, f32[768,352]{0,1:T(8,128)} %fusion.5), kind=kOutput, calls=%fused_computation.3 | convolution fusion | flops 2217787392 | bytes 10256384 | tf_op jit(solution)/shard_map/dot_general | solution.py:142
  224.9 4.6 %all-to-all-start.1 = ((bf16[8,96,2048]{2,1,0:T(8,128)(2,1)}), bf16[8,96,2048]{2,1,0:T(8,128)(2,1)}, u32[]{:S(2)}, u32[]{:S(2)}) async-start(bf16[8,96,2048]{2,1,0:T(8,128)(2,1)} %bitcast.110), calls=%async_computation.2 | async-start | bytes 6291456 | tf_op jit(solution)/shard_map/all_to_all | solution.py:145
  229.6 0.5 all-gather.9.cloned.1.call-update
  230.1 0.2 reduce-scatter.5.cloned.1.call-start
  230.4 0.5 slice_bitcast_fusion.3
  230.9 0.3 fusion.22
  231.2 3.5 fusion.63
  234.7 93.1 %all-to-all-done.1 = bf16[8,96,2048]{2,1,0:T(8,128)(2,1)} async-done(((bf16[8,96,2048]{2,1,0:T(8,128)(2,1)}), bf16[8,96,2048]{2,1,0:T(8,128)(2,1)}, u32[]{:S(2)}, u32[]{:S(2)}) %all-to-all-start.1) | async-done | bytes 3145760 | tf_op jit(solution)/shard_map/all_to_all | solution.py:145
  327.7 7.5 %gather_fusion.1 = bf16[512,2048]{1,0:T(8,128)(2,1)} fusion(bf16[768,2048]{1,0:T(8,128)(2,1)} %bitcast.21, s32[1024]{0:T(1024)S(1)} %pad_clamp_fusion), kind=kCustom, calls=%fused_computation.1 | custom fusion | bytes 4196352 | tf_op jit(solution)/shard_map/gather | solution.py:152
  335.3 2.7 reshape.220
  338.0 4.5 %fusion.61 = (bf16[128,1,2048]{2,1,0:T(2,128)(2,1)}, bf16[128,1,2048]{2,1,0:T(2,128)(2,1)}, bf16[128,1,2048]{2,1,0:T(2,128)(2,1)}, bf16[128,1,2048]{2,1,0:T(2,128)(2,1)}) fusion(bf16[128,4,2048]{2,1,0:T(4,128)(2,1)S(1)} %reshape.220), kind=kLoop, calls=%fused_computation.116 | loop fusion | bytes 4194304 | tf_op jit(solution)/shard_map/slice | solution.py:157
  342.5 27.7 %all-gather.9.cloned.1.call-done = bf16[2048,704]{0,1:T(8,128)(2,1)} async-done(((bf16[256,704]{0,1:T(8,128)(2,1)}), bf16[2048,704]{0,1:T(8,128)(2,1)}) %all-gather.9.cloned.1.call-update) | async-done | bytes 2883600 | tf_op jit(solution)/shard_map/all_gather | solution.py:111
  370.2 8.1 %fusion.1 = bf16[128,2048]{1,0:T(8,128)(2,1)} fusion(bf16[704,2048]{1,0:T(8,128)(2,1)} %all-gather.11.cloned.1.call-done, bf16[128,2048]{1,0:T(8,128)(2,1)} %copy-done.1, bf16[2048,704]{0,1:T(8,128)(2,1)} %all-gather.9.cloned.1.call-done, bf16[128,1,2048]{2,1,0:T(2,128)(2,1)} %get-tuple-element.11, bf16[128,1,2048]{2,1,0:T(2,128)(2,1)} %get-tuple-element.9, ...), kind=kOutput, calls=%fused_computation.6 | convolution fusion | flops 742408192 | bytes 9275904 | tf_op jit(solution)/shard_map/dot_general | solution.py:115
  378.3 0.7 copy.48
  379.1 19.2 %reduce-scatter.5.cloned.1.call-done = bf16[128,512]{1,0:T(8,128)(2,1)} async-done(((bf16[128,2048]{1,0:T(8,128)(2,1)}), bf16[128,512]{1,0:T(8,128)(2,1)}) %reduce-scatter.5.cloned.1.call-update) | async-done | bytes 131088 | tf_op jit(solution)/shard_map/reduce_scatter | solution.py:161
  398.3 1.6 fusion.44
  (53 shorter events, 0.5 us)
Async XLA Ops:
  7.2 209.8 %copy-start = (bf16[1,352,2048]{2,1,0:T(8,128)(2,1)S(1)}, bf16[1,352,2048]{2,1,0:T(8,128)(2,1)}, u32[]{:S(2)}) copy-start(bf16[1,352,2048]{2,1,0:T(8,128)(2,1)} %param.31) | copy-start | bytes 4325380
  7.2 58.9 %all-gather.5.cloned.1.call-start = ((), (), s32[]{:S(2)}) async-start(), calls=%async_computation.4 | async-start | bytes 1179648 | tf_op jit(solution)/shard_map/all_gather | solution.py:89
  9.9 8.8 %collective-permute-start = (bf16[2,128,256]{1,2,0:T(8,128)(2,1)S(1)}, bf16[2,128,256]{1,2,0:T(8,128)(2,1)S(1)}, u32[]{:S(2)}, u32[]{:S(2)}) collective-permute-start(bf16[2,128,256]{1,2,0:T(8,128)(2,1)S(1)} %get-tuple-element.14), channel_id=1, source_target_pairs={{0,28},{4,0},{8,4},{12,8},{16,12},{20,16},{24,20},{28,24},{1,29},{... | collective-permute-start | bytes 393224 | tf_op jit(solution)/shard_map/ppermute | solution.py:55
  16.0 76.4 %reduce-scatter.3.cloned.1.call-start = ((), (), s32[]{:S(2)}) async-start(), calls=%async_computation.5 | async-start | bytes 655360 | tf_op jit(solution)/shard_map/reduce_scatter | solution.py:92
  18.7 10.4 %collective-permute-start.1 = (bf16[2,256,256]{1,2,0:T(8,128)(2,1)S(1)}, bf16[2,256,256]{1,2,0:T(8,128)(2,1)S(1)}, u32[]{:S(2)}, u32[]{:S(2)}) collective-permute-start(bf16[2,256,256]{1,2,0:T(8,128)(2,1)S(1)} %pad_maximum_fusion.1), channel_id=1, source_target_pairs={{0,24},{4,28},{8,0},{12,4},{16,8},{20,12},{24,16},{28,20},{1,25},{... | collective-permute-start | bytes 786440 | tf_op jit(solution)/shard_map/ppermute | solution.py:55
  29.2 23.8 %collective-permute-start.2 = (bf16[2,512,256]{1,2,0:T(8,128)(2,1)S(1)}, bf16[2,512,256]{1,2,0:T(8,128)(2,1)S(1)}, u32[]{:S(2)}, u32[]{:S(2)}) collective-permute-start(bf16[2,512,256]{1,2,0:T(8,128)(2,1)S(1)} %pad_maximum_fusion), channel_id=1, source_target_pairs={{0,16},{4,20},{8,24},{12,28},{16,0},{20,4},{24,8},{28,12},{1,17},{... | collective-permute-start | bytes 1572872 | tf_op jit(solution)/shard_map/ppermute | solution.py:55
  53.9 4.3 %copy-start.7 = (bf16[128,256]{1,0:T(8,128)(2,1)S(1)}, bf16[128,256]{1,0:T(8,128)(2,1)}, u32[]{:S(2)}) copy-start(bf16[128,256]{1,0:T(8,128)(2,1)} %param.17) | copy-start | bytes 196612
  56.9 1.7 copy-start.10
  59.0 10.2 %copy-start.8 = (s32[128,4]{0,1:T(4,128)S(1)}, s32[128,4]{0,1:T(4,128)}, u32[]{:S(2)}) copy-start(s32[128,4]{0,1:T(4,128)} %param.32) | copy-start | bytes 6148
  59.0 10.5 %copy-start.12 = (bf16[512]{0:T(512)(128)(2,1)S(1)}, bf16[512]{0:T(512)(128)(2,1)}, u32[]{:S(2)}) copy-start(bf16[512]{0:T(512)(128)(2,1)} %param.24) | copy-start | bytes 3076
  59.4 9.1 %copy-start.5 = (bf16[128,2,128]{0,2,1:T(8,128)(2,1)}, bf16[128,2,128]{0,2,1:T(8,128)(2,1)S(1)}, u32[]{:S(2)}) copy-start(bf16[128,2,128]{0,2,1:T(8,128)(2,1)S(1)} %fusion.18) | copy-start | bytes 196612
  59.4 33.0 %copy-start.2 = (bf16[128,512]{1,0:T(8,128)(2,1)S(1)}, bf16[128,512]{1,0:T(8,128)(2,1)}, u32[]{:S(2)}) copy-start(bf16[128,512]{1,0:T(8,128)(2,1)} %param.22) | copy-start | bytes 393220
  68.4 162.8 %all-gather.7.cloned.1.call-start = ((), (), s32[]{:S(2)}) async-start(), calls=%async_computation.6 | async-start | bytes 3244032 | tf_op jit(solution)/shard_map/all_gather | solution.py:106
  107.5 123.7 %copy-start.1 = (bf16[128,2048]{1,0:T(8,128)(2,1)}, bf16[128,2048]{1,0:T(8,128)(2,1)S(1)}, u32[]{:S(2)}) copy-start(bf16[128,2048]{1,0:T(8,128)(2,1)S(1)} %all_gather.16) | copy-start | bytes 1572868
  111.8 100.4 %all-to-all-start = ((bf16[8,96,2048]{2,1,0:T(8,128)(2,1)}), bf16[8,96,2048]{2,1,0:T(8,128)(2,1)}, u32[]{:S(2)}, u32[]{:S(2)}) async-start(bf16[8,96,2048]{2,1,0:T(8,128)(2,1)} %bitcast.109), calls=%async_computation.1 | async-start | bytes 6291456 | tf_op jit(solution)/shard_map/all_to_all | solution.py:136
  117.3 225.2 %all-gather.11.cloned.1.call-start = ((), (), s32[]{:S(2)}) async-start(), calls=%async_computation.8 | async-start | bytes 3244032 | tf_op jit(solution)/shard_map/all_gather | solution.py:117
  224.9 5.4 %copy-start.9 = (bf16[2048]{0:T(1024)(128)(2,1)S(1)}, bf16[2048]{0:T(1024)(128)(2,1)}, u32[]{:S(2)}) copy-start(bf16[2048]{0:T(1024)(128)(2,1)} %param.28) | copy-start | bytes 12292
  224.9 5.4 %copy-start.11 = (f32[128,4]{0,1:T(4,128)S(1)}, f32[128,4]{0,1:T(4,128)}, u32[]{:S(2)}) copy-start(f32[128,4]{0,1:T(4,128)} %param.33) | copy-start | bytes 6148
  224.9 102.8 %all-to-all-start.1 = ((bf16[8,96,2048]{2,1,0:T(8,128)(2,1)}), bf16[8,96,2048]{2,1,0:T(8,128)(2,1)}, u32[]{:S(2)}, u32[]{:S(2)}) async-start(bf16[8,96,2048]{2,1,0:T(8,128)(2,1)} %bitcast.110), calls=%async_computation.2 | async-start | bytes 6291456 | tf_op jit(solution)/shard_map/all_to_all | solution.py:145
  229.5 140.7 %all-gather.9.cloned.1.call-start = ((), (), s32[]{:S(2)}) async-start(), calls=%async_computation.7 | async-start | bytes 3244032 | tf_op jit(solution)/shard_map/all_gather | solution.py:111
  230.1 168.2 %reduce-scatter.5.cloned.1.call-start = ((), (), s32[]{:S(2)}) async-start(), calls=%async_computation.9 | async-start | bytes 655360 | tf_op jit(solution)/shard_map/reduce_scatter | solution.py:161
  370.2 8.1 %copy-start.6 = (bf16[128,2,128]{0,2,1:T(8,128)(2,1)S(1)}, bf16[128,2,128]{0,2,1:T(8,128)(2,1)}, u32[]{:S(2)}) copy-start(bf16[128,2,128]{0,2,1:T(8,128)(2,1)} %copy-done.5) | copy-start | bytes 196612
  370.2 28.1 %copy-start.3 = (bf16[128,512]{1,0:T(8,128)(2,1)S(1)}, bf16[128,512]{1,0:T(8,128)(2,1)}, u32[]{:S(2)}) copy-start(bf16[128,512]{1,0:T(8,128)(2,1)} %param.22) | copy-start | bytes 393220
  370.2 28.1 %copy-start.4 = (bf16[128,512]{1,0:T(8,128)(2,1)S(1)}, bf16[128,512]{1,0:T(8,128)(2,1)}, u32[]{:S(2)}) copy-start(bf16[128,512]{1,0:T(8,128)(2,1)} %reduce-scatter.3.cloned.1.call-done) | copy-start | bytes 393220
Sparse Core Ops, SparseCore 0:
  16.1 49.9 all-gather.4
  68.5 23.7 reduce-scatter.2
  94.6 109.6 all-gather.6
  206.4 102.8 all-gather.10
  311.4 58.7 all-gather.8
  378.4 19.8 reduce-scatter.4
